TPU v7x, 256 devices: a whole 4x4x8 slice. The times are simulated.
256 devices in a mesh: ops: 4 (over y), blk: 64 (over x, z, core).
Axes of the slice: x: 4, y: 4, z: 8, core: 2. Of those that a mesh axis runs over, the one named last changes fastest.
Arguments:
- psi: bfloat16 [16384, 8192], P('blk'), may hold values from -6 to 6
- left_env: bfloat16 [16, 64, 256, 256], P('ops', 'blk'), may hold values from -0.09375 to 0.09375
- right_env: bfloat16 [16, 64, 128, 128], P('ops', 'blk'), may hold values from -0.5 to 0.5
- left_live: int32 [64], replicated, may hold values from 64 to 256, as said below
- right_live: int32 [64], replicated, may hold values from 32 to 128, as said below
Outputs:
- hpsi: float32 [16384, 8192], P('blk', 'ops')
Inputs may be any that keep to these rules, and one draw needn't show every extreme that they name: `left_live`: some left sector is fully live. `right_live`: some right sector is fully live.
All inputs are finite; a program needn't handle non-finite values.
Results may differ from a plain program's by a relative error of at most 0.0029.
Values may be sent and summed in bfloat16 or wider, within the bound.
No kernel may reach another device: no remote copies, remote signals or barrier semaphores. Data moves between devices by JAX's collectives and lax.ppermute only.
A program may use at most 128 MiB of HBM per device.

v0:
```python
import jax
import jax.numpy as jnp
from jax import lax
from jax.sharding import PartitionSpec as P


def shards(psi, left_env, right_env, left_live, right_live):
    sectors = lax.axis_size("blk")
    rows = psi.shape[0]
    columns = psi.shape[1]
    width = columns // sectors
    mine = lax.axis_index("blk")
    row_live = lax.dynamic_index_in_dim(left_live, mine, keepdims=False)
    row_mask = jnp.arange(rows, dtype=jnp.int32) < row_live
    col_mask = (jnp.arange(width, dtype=jnp.int32)[None, :] < right_live[:, None]).reshape(columns)
    masked = jnp.where(row_mask[:, None] & col_mask[None, :], psi, jnp.zeros_like(psi))
    groups = lax.axis_size("ops")
    share = columns // groups
    share_start = lax.axis_index("ops") * share
    share_mask = lax.dynamic_slice_in_dim(col_mask, share_start, share)
    terms = left_env.shape[0]
    lefts = left_env[:, 0]
    rights = lax.all_gather(right_env, "blk", axis=1, tiled=True)
    partial_value = jnp.zeros((rows, sectors, width), jnp.float32)
    for t in range(terms):
        mixed = jnp.dot(lefts[t], masked, preferred_element_type=jnp.float32).astype(jnp.bfloat16)
        mixed = mixed.reshape(rows, sectors, width)
        partial_value = partial_value + jnp.einsum(
            "ajr,jsr->ajs", mixed, rights[t], preferred_element_type=jnp.float32
        )
    partial_value = partial_value.reshape(rows, columns)
    summed = lax.psum_scatter(partial_value, "ops", scatter_dimension=1, tiled=True)
    return jnp.where(row_mask[:, None] & share_mask[None, :], summed, jnp.zeros_like(summed))


def solution(mesh):
    in_specs = (P("blk", None), P("ops", "blk", None, None), P("ops", "blk", None, None), P(), P())
    out_specs = P("blk", "ops")
    return jax.shard_map(shards, mesh=mesh, in_specs=in_specs, out_specs=out_specs, check_vma=False)
```

profile of v0, /device:TPU:1, one launch (start us, length us, event | category | flops | bytes accessed | tf_op | source)
XLA Modules:
  0.0 224.4 jit_solution(11705806541663982912)
XLA Ops:
  6.5 0.0 all-gather.2.cloned.1.call-start
  6.5 0.7 all-gather.2.cloned.1.call-update
  7.3 0.0 reduce-scatter.2.cloned.1.call-start
  7.3 1.2 dynamic_slice.7
  8.5 0.6 iota_compare_fusion.1
  9.2 0.7 fusion.11
  9.9 0.0 copy-start.3
  10.0 0.0 copy-start.4
  10.0 6.2 %convolution_convert_fusion.2 = bf16[8192,256]{1,0:T(8,128)(2,1)} fusion(bf16[4,1,256,256]{3,2,1,0:T(8,128)(2,1)} %param.6, bf16[256,8192]{1,0:T(8,128)(2,1)} %param.5, pred[8192]{0:T(1024)(128)(4,1)S(1)} %fusion.11, pred[256]{0:T(512)(128)(4,1)S(1)} %iota_compare_fusion.1), kind=kOutput, calls=%fused_computation.2 | convolution fusion | flops 1080033280 | bytes 8528128 | tf_op jit(solution)/shard_map/dot_general | solution.py:26
  16.2 0.0 copy-done.3
  16.2 0.0 copy-done.4
  16.2 4.2 %convolution_convert_fusion.3 = bf16[8192,256]{1,0:T(8,128)(2,1)} fusion(bf16[4,1,256,256]{3,2,1,0:T(8,128)(2,1)S(1)} %copy-done.4, bf16[256,8192]{1,0:T(8,128)(2,1)S(1)} %copy-done.3, pred[8192]{0:T(1024)(128)(4,1)S(1)} %fusion.11, pred[256]{0:T(512)(128)(4,1)S(1)} %iota_compare_fusion.1), kind=kOutput, calls=%fused_computation.3 | convolution fusion | flops 1080033280 | bytes 8528384 | tf_op jit(solution)/shard_map/dot_general | solution.py:26
  20.3 4.1 %convolution_convert_fusion.1 = bf16[8192,256]{1,0:T(8,128)(2,1)} fusion(bf16[4,1,256,256]{3,2,1,0:T(8,128)(2,1)S(1)} %copy-done.4, bf16[256,8192]{1,0:T(8,128)(2,1)S(1)} %copy-done.3, pred[8192]{0:T(1024)(128)(4,1)S(1)} %fusion.11, pred[256]{0:T(512)(128)(4,1)S(1)} %iota_compare_fusion.1), kind=kOutput, calls=%fused_computation.1 | convolution fusion | flops 1080033280 | bytes 8528384 | tf_op jit(solution)/shard_map/dot_general | solution.py:26
  24.5 4.1 %convolution_convert_fusion = bf16[8192,256]{1,0:T(8,128)(2,1)} fusion(bf16[4,1,256,256]{3,2,1,0:T(8,128)(2,1)S(1)} %copy-done.4, bf16[256,8192]{1,0:T(8,128)(2,1)S(1)} %copy-done.3, pred[8192]{0:T(1024)(128)(4,1)S(1)} %fusion.11, pred[256]{0:T(512)(128)(4,1)S(1)} %iota_compare_fusion.1), kind=kOutput, calls=%fused_computation | convolution fusion | flops 1080033280 | bytes 8528384 | tf_op jit(solution)/shard_map/dot_general | solution.py:26
  28.6 68.6 %all-gather.2.cloned.1.call-done = bf16[4,64,128,128]{3,2,1,0:T(8,128)(2,1)} async-done(((bf16[4,1,128,128]{3,2,1,0:T(8,128)(2,1)}), bf16[4,64,128,128]{3,2,1,0:T(8,128)(2,1)}) %all-gather.2.cloned.1.call-update) | async-done | bytes 8388624 | tf_op jit(solution)/shard_map/all_gather | solution.py:23
  97.2 0.0 copy-start
  97.2 0.0 copy-start.2
  97.2 4.2 %fusion.1 = f32[64,256,128]{1,2,0:T(8,128)S(1)} fusion(bf16[256,64,128]{0,2,1:T(8,128)(2,1)} %bitcast.50, bf16[4,64,128,128]{3,2,1,0:T(8,128)(2,1)} %all-gather.2.cloned.1.call-done), kind=kOutput, calls=%fused_computation.10 | convolution fusion | flops 536870912 | bytes 14680064 | tf_op jit(solution)/shard_map/ajr,jsr->ajs/dot_general | solution.py:28
  101.5 1.0 copy-done
  102.5 1.2 copy-done.2
  103.7 0.0 copy-start.1
  103.7 4.5 %fusion.2 = f32[64,256,128]{1,2,0:T(8,128)} fusion(bf16[256,64,128]{0,2,1:T(8,128)(2,1)S(1)} %bitcast.49, bf16[4,64,128,128]{3,2,1,0:T(8,128)(2,1)S(1)} %copy-done), kind=kOutput, calls=%fused_computation.12 | convolution fusion | flops 536870912 | bytes 14680064 | tf_op jit(solution)/shard_map/ajr,jsr->ajs/dot_general | solution.py:28
  108.1 0.0 copy-done.1
  108.1 4.5 %fusion = f32[64,256,128]{1,2,0:T(8,128)} fusion(bf16[256,64,128]{0,2,1:T(8,128)(2,1)S(1)} %bitcast.48, bf16[4,64,128,128]{3,2,1,0:T(8,128)(2,1)S(1)} %copy-done), kind=kOutput, calls=%fused_computation.8 | convolution fusion | flops 536870912 | bytes 14680064 | tf_op jit(solution)/shard_map/ajr,jsr->ajs/dot_general | solution.py:28
  112.6 13.2 %add_add_fusion = f32[64,256,128]{1,2,0:T(8,128)} fusion(f32[64,256,128]{1,2,0:T(8,128)} %fusion, f32[64,256,128]{1,2,0:T(8,128)} %fusion.2, f32[64,256,128]{1,2,0:T(8,128)S(1)} %fusion.1, bf16[256,64,128]{0,2,1:T(8,128)(2,1)} %bitcast.47, bf16[4,64,128,128]{3,2,1,0:T(8,128)(2,1)} %all-gather.2.cloned.1.call-done), kind=kOutput, calls=%fused_computation.4 | convolution fusion | flops 543162368 | bytes 39845888 | tf_op jit(solution)/shard_map/ajr,jsr->ajs/dot_general | solution.py:28
  125.8 8.9 %copy.10 = f32[256,8192]{1,0:T(8,128)} copy(f32[256,8192]{0,1:T(8,128)} %bitcast.46) | data formatting | bytes 16777216 | tf_op jit(solution)/shard_map/reshape | solution.py:31
  134.7 0.0 reduce-scatter.2.cloned.1.call-update
  134.8 79.6 %reduce-scatter.2.cloned.1.call-done = f32[256,2048]{1,0:T(8,128)} async-done(((f32[256,8192]{1,0:T(8,128)}), f32[256,2048]{1,0:T(8,128)}) %reduce-scatter.2.cloned.1.call-update) | async-done | bytes 2097168 | tf_op jit(solution)/shard_map/reduce_scatter | solution.py:32
  214.4 3.2 %and_select_fusion.1 = f32[256,2048]{1,0:T(8,128)} fusion(f32[256,2048]{1,0:T(8,128)} %reduce-scatter.2.cloned.1.call-done, pred[2048]{0:T(1024)(128)(4,1)S(1)} %dynamic_slice.8, pred[256]{0:T(512)(128)(4,1)S(1)} %iota_compare_fusion.1), kind=kLoop, calls=%fused_computation.13 | loop fusion | flops 1048576 | bytes 4196608 | tf_op jit(solution)/shard_map/jit(_where)/select_n | solution.py:33
  (1 shorter events, 0.0 us)
Async XLA Ops:
  6.5 90.7 %all-gather.2.cloned.1.call-start = ((), (), s32[]{:S(2)}) async-start(), calls=%async_computation.1 | async-start | bytes 8519680 | tf_op jit(solution)/shard_map/all_gather | solution.py:23
  7.3 207.1 %reduce-scatter.2.cloned.1.call-start = ((), (), s32[]{:S(2)}) async-start(), calls=%async_computation.2 | async-start | bytes 10485760 | tf_op jit(solution)/shard_map/reduce_scatter | solution.py:32
  9.9 6.2 %copy-start.3 = (bf16[256,8192]{1,0:T(8,128)(2,1)S(1)}, bf16[256,8192]{1,0:T(8,128)(2,1)}, u32[]{:S(2)}) copy-start(bf16[256,8192]{1,0:T(8,128)(2,1)} %param.5) | copy-start | bytes 12582916
  10.0 6.2 %copy-start.4 = (bf16[4,1,256,256]{3,2,1,0:T(8,128)(2,1)S(1)}, bf16[4,1,256,256]{3,2,1,0:T(8,128)(2,1)}, u32[]{:S(2)}) copy-start(bf16[4,1,256,256]{3,2,1,0:T(8,128)(2,1)} %param.6) | copy-start | bytes 1572868
  97.2 5.2 %copy-start = (bf16[4,64,128,128]{3,2,1,0:T(8,128)(2,1)S(1)}, bf16[4,64,128,128]{3,2,1,0:T(8,128)(2,1)}, u32[]{:S(2)}) copy-start(bf16[4,64,128,128]{3,2,1,0:T(8,128)(2,1)} %all-gather.2.cloned.1.call-done) | copy-start | bytes 25165828
  97.2 6.4 %copy-start.2 = (bf16[8192,256]{1,0:T(8,128)(2,1)S(1)}, bf16[8192,256]{1,0:T(8,128)(2,1)}, u32[]{:S(2)}) copy-start(bf16[8192,256]{1,0:T(8,128)(2,1)} %convolution_convert_fusion.3) | copy-start | bytes 12582916
  103.7 4.5 %copy-start.1 = (bf16[8192,256]{1,0:T(8,128)(2,1)S(1)}, bf16[8192,256]{1,0:T(8,128)(2,1)}, u32[]{:S(2)}) copy-start(bf16[8192,256]{1,0:T(8,128)(2,1)} %convolution_convert_fusion.1) | copy-start | bytes 12582916
Sparse Core Ops, SparseCore 0:
  10.1 87.0 all-gather.1
  134.9 79.4 reduce-scatter.1
where the time goes:
time: 225 us; the launch traced here: 224 us
  waiting for transfers between devices  149 us (66%)
  matrix products  45 us (20%)
  between operations  13.5 us (6%)
  local copies, waits for them, and re-layouts  12.4 us (6%)
  other arithmetic  4.57 us (2%)
    reduce_scatter x1, waiting for transfers between devices, shards(): lax.psum_scatter(partial_value, 'ops', scatter_dimension=1, tiled=True)  79.6 us
    all_gather x1, waiting for transfers between devices, shards(): rights = lax.all_gather(right_env, 'blk', axis=1, tiled=True)  68.6 us
    dot_general x4, matrix products, shards(): jnp.einsum('ajr,jsr->ajs', mixed, rights[t], preferred_element_type=jnp.f...  26.4 us
    dot_general x4, matrix products, shards(): jnp.dot(lefts[t], masked, preferred_element_type=jnp.float32)  18.6 us
    reshape x1, local copies, waits for them, and re-layouts, shards(): partial_value = partial_value.reshape(rows, columns)  8.9 us
  transfers between devices with their start and end apart: 2, of which 2 were waited for; matrix products, arithmetic and copies ran while one was open for 9% of the time, Pallas kernels for 0%

commit v1 on v0

--- a/solution.py
+++ b/solution.py
@@ -20,7 +20,9 @@
     share_mask = lax.dynamic_slice_in_dim(col_mask, share_start, share)
     terms = left_env.shape[0]
     lefts = left_env[:, 0]
-    rights = lax.all_gather(right_env, "blk", axis=1, tiled=True)
+    rights = jnp.concatenate(
+        lax.all_to_all(jnp.stack([right_env] * lax.axis_size("blk")), "blk", 0, 0), axis=1
+    )
     partial_value = jnp.zeros((rows, sectors, width), jnp.float32)
     for t in range(terms):
         mixed = jnp.dot(lefts[t], masked, preferred_element_type=jnp.float32).astype(jnp.bfloat16)

time: 225 us -> 350 us (1.56)
  waiting for transfers between devices: 149 us -> 245 us
  local copies, waits for them, and re-layouts: 12.4 us -> 28.3 us
  starting transfers between devices: 0.04 us -> 13.5 us
    all_to_all x0 -> x1, waiting for transfers between devices: none -> 166 us  [shards(): lax.all_to_all(jnp.stack([right_env] * lax.axis_size('blk')), 'blk', 0, 0)]
    all_gather x1 -> x0, waiting for transfers between devices: 68.6 us -> none  [shards(): rights = lax.all_gather(right_env, 'blk', axis=1, tiled=True)]
    all_to_all x0 -> x1, starting transfers between devices: none -> 13.3 us  [shards(): lax.all_to_all(jnp.stack([right_env] * lax.axis_size('blk')), 'blk', 0, 0)]
    all_to_all x0 -> x1, local copies, waits for them, and re-layouts: none -> 10.3 us  [shards(): lax.all_to_all(jnp.stack([right_env] * lax.axis_size('blk')), 'blk', 0, 0)]
    another operation x0 -> x1, local copies, waits for them, and re-layouts: none -> 6.26 us  [shards(): jnp.stack([right_env] * lax.axis_size('blk'))]
  transfers between devices with their start and end apart: 2 -> 2, of which waited for: 2 -> 2; matrix products, arithmetic and copies ran while one was open for 9% -> 6% of each run, Pallas kernels for 0% -> 0%
where the time goes in v1:
time: 350 us
  waiting for transfers between devices  245 us (70%)
  matrix products  45.2 us (13%)
  local copies, waits for them, and re-layouts  28.3 us (8%)
  starting transfers between devices  13.5 us (4%)
  between operations  13.5 us (4%)
  other arithmetic  3.92 us (1%)
    all_to_all x1, waiting for transfers between devices, shards(): lax.all_to_all(jnp.stack([right_env] * lax.axis_size('blk')), 'blk', 0, 0)  166 us
    reduce_scatter x1, waiting for transfers between devices, shards(): lax.psum_scatter(partial_value, 'ops', scatter_dimension=1, tiled=True)  79.8 us
    dot_general x4, matrix products, shards(): jnp.einsum('ajr,jsr->ajs', mixed, rights[t], preferred_element_type=jnp.f...  26.6 us
    dot_general x4, matrix products, shards(): jnp.dot(lefts[t], masked, preferred_element_type=jnp.float32)  18.6 us
    all_to_all x1, starting transfers between devices, shards(): lax.all_to_all(jnp.stack([right_env] * lax.axis_size('blk')), 'blk', 0, 0)  13.3 us
    all_to_all x1, local copies, waits for them, and re-layouts, shards(): lax.all_to_all(jnp.stack([right_env] * lax.axis_size('blk')), 'blk', 0, 0)  10.3 us
    reshape x1, local copies, waits for them, and re-layouts, shards(): partial_value = partial_value.reshape(rows, columns)  8.91 us
  transfers between devices with their start and end apart: 2, of which 2 were waited for; matrix products, arithmetic and copies ran while one was open for 6% of the time, Pallas kernels for 0%

profile of v1, /device:TPU:1, one launch (start us, length us, event | category | flops | bytes accessed | tf_op | source)
XLA Modules:
  0.0 349.8 jit_solution(13419207221584529534)
XLA Ops:
  6.5 6.3 %stack.2 = bf16[64,4,1,128,128]{4,3,2,1,0:T(8,128)(2,1)} broadcast(bf16[4,128,128]{2,1,0:T(8,128)(2,1)} %bitcast.59), dimensions={1,3,4} | broadcast | bytes 8519680 | tf_op jit(solution)/shard_map/stack | solution.py:24
  12.8 0.0 copy-start.6
  12.8 0.0 copy-start.3
  12.8 0.0 copy-start.5
  12.8 13.3 %all-to-all-start = ((bf16[64,4,1,128,128]{4,3,2,1,0:T(8,128)(2,1)}), bf16[64,4,1,128,128]{4,3,2,1,0:T(8,128)(2,1)}, u32[]{:S(2)}, u32[]{:S(2)}) async-start(bf16[64,4,1,128,128]{4,3,2,1,0:T(8,128)(2,1)} %stack.2), calls=%async_computation | async-start | bytes 16777216 | tf_op jit(solution)/shard_map/all_to_all | solution.py:24
  26.1 0.2 reduce-scatter.2.cloned.1.call-start
  26.3 0.0 copy-done.6
  26.3 0.6 dynamic_slice.7
  26.9 0.6 iota_compare_fusion.1
  27.6 0.0 copy-done.3
  27.6 0.1 fusion.11
  27.7 0.0 copy-done.5
  27.7 0.0 copy-start.4
  27.7 6.2 %convolution_convert_fusion.2 = bf16[8192,256]{1,0:T(8,128)(2,1)} fusion(bf16[4,1,256,256]{3,2,1,0:T(8,128)(2,1)S(1)} %copy-done.5, bf16[256,8192]{1,0:T(8,128)(2,1)} %param.5, pred[8192]{0:T(1024)(128)(4,1)S(1)} %fusion.11, pred[256]{0:T(512)(128)(4,1)S(1)} %iota_compare_fusion.1), kind=kOutput, calls=%fused_computation.2 | convolution fusion | flops 1080033280 | bytes 8528384 | tf_op jit(solution)/shard_map/dot_general | solution.py:28
  33.9 0.0 copy-done.4
  33.9 4.1 %convolution_convert_fusion.3 = bf16[8192,256]{1,0:T(8,128)(2,1)} fusion(bf16[4,1,256,256]{3,2,1,0:T(8,128)(2,1)S(1)} %copy-done.5, bf16[256,8192]{1,0:T(8,128)(2,1)S(1)} %copy-done.4, pred[8192]{0:T(1024)(128)(4,1)S(1)} %fusion.11, pred[256]{0:T(512)(128)(4,1)S(1)} %iota_compare_fusion.1), kind=kOutput, calls=%fused_computation.3 | convolution fusion | flops 1080033280 | bytes 8528384 | tf_op jit(solution)/shard_map/dot_general | solution.py:28
  38.0 4.1 %convolution_convert_fusion.1 = bf16[8192,256]{1,0:T(8,128)(2,1)} fusion(bf16[4,1,256,256]{3,2,1,0:T(8,128)(2,1)S(1)} %copy-done.5, bf16[256,8192]{1,0:T(8,128)(2,1)S(1)} %copy-done.4, pred[8192]{0:T(1024)(128)(4,1)S(1)} %fusion.11, pred[256]{0:T(512)(128)(4,1)S(1)} %iota_compare_fusion.1), kind=kOutput, calls=%fused_computation.1 | convolution fusion | flops 1080033280 | bytes 8528384 | tf_op jit(solution)/shard_map/dot_general | solution.py:28
  42.2 4.2 %convolution_convert_fusion = bf16[8192,256]{1,0:T(8,128)(2,1)} fusion(bf16[4,1,256,256]{3,2,1,0:T(8,128)(2,1)S(1)} %copy-done.5, bf16[256,8192]{1,0:T(8,128)(2,1)S(1)} %copy-done.4, pred[8192]{0:T(1024)(128)(4,1)S(1)} %fusion.11, pred[256]{0:T(512)(128)(4,1)S(1)} %iota_compare_fusion.1), kind=kOutput, calls=%fused_computation | convolution fusion | flops 1080033280 | bytes 8528384 | tf_op jit(solution)/shard_map/dot_general | solution.py:28
  46.3 165.5 %all-to-all-done = bf16[64,4,1,128,128]{4,3,2,1,0:T(8,128)(2,1)} async-done(((bf16[64,4,1,128,128]{4,3,2,1,0:T(8,128)(2,1)}), bf16[64,4,1,128,128]{4,3,2,1,0:T(8,128)(2,1)}, u32[]{:S(2)}, u32[]{:S(2)}) %all-to-all-start) | async-done | bytes 8388640 | tf_op jit(solution)/shard_map/all_to_all | solution.py:24
  211.8 10.3 %copy.22 = bf16[64,4,1,128,128]{4,3,0,2,1:T(8,128)(2,1)} copy(bf16[64,4,1,128,128]{4,3,2,1,0:T(8,128)(2,1)} %all-to-all-done) | data formatting | bytes 16777216 | tf_op jit(solution)/shard_map/all_to_all | solution.py:24
  222.2 0.0 copy-start
  222.2 0.0 copy-start.2
  222.2 4.2 %fusion.1 = f32[64,256,128]{1,2,0:T(8,128)S(1)} fusion(bf16[256,64,128]{0,2,1:T(8,128)(2,1)} %bitcast.58, bf16[4,64,1,128,128]{4,3,1,2,0:T(8,128)(2,1)} %bitcast.50), kind=kOutput, calls=%fused_computation.11 | convolution fusion | flops 536870912 | bytes 14680064 | tf_op jit(solution)/shard_map/ajr,jsr->ajs/dot_general | solution.py:30
  226.4 1.0 copy-done
  227.4 1.2 copy-done.2
  228.6 0.0 copy-start.1
  228.6 4.5 %fusion.2 = f32[64,256,128]{1,2,0:T(8,128)} fusion(bf16[256,64,128]{0,2,1:T(8,128)(2,1)S(1)} %bitcast.57, bf16[4,64,1,128,128]{4,3,1,2,0:T(8,128)(2,1)S(1)} %bitcast.52), kind=kOutput, calls=%fused_computation.13 | convolution fusion | flops 536870912 | bytes 14680064 | tf_op jit(solution)/shard_map/ajr,jsr->ajs/dot_general | solution.py:30
  233.1 0.0 copy-done.1
  233.1 4.7 %fusion = f32[64,256,128]{1,2,0:T(8,128)} fusion(bf16[256,64,128]{0,2,1:T(8,128)(2,1)S(1)} %bitcast.56, bf16[4,64,1,128,128]{4,3,1,2,0:T(8,128)(2,1)S(1)} %bitcast.53), kind=kOutput, calls=%fused_computation.9 | convolution fusion | flops 536870912 | bytes 14680064 | tf_op jit(solution)/shard_map/ajr,jsr->ajs/dot_general | solution.py:30
  237.8 13.2 %add_add_fusion = f32[64,256,128]{1,2,0:T(8,128)} fusion(f32[64,256,128]{1,2,0:T(8,128)} %fusion, f32[64,256,128]{1,2,0:T(8,128)} %fusion.2, f32[64,256,128]{1,2,0:T(8,128)S(1)} %fusion.1, bf16[256,64,128]{0,2,1:T(8,128)(2,1)} %bitcast.55, bf16[4,64,1,128,128]{4,3,1,2,0:T(8,128)(2,1)} %bitcast.51), kind=kOutput, calls=%fused_computation.5 | convolution fusion | flops 543162368 | bytes 39845888 | tf_op jit(solution)/shard_map/ajr,jsr->ajs/dot_general | solution.py:30
  251.0 8.9 %copy.16 = f32[256,8192]{1,0:T(8,128)} copy(f32[256,8192]{0,1:T(8,128)} %bitcast.54) | data formatting | bytes 16777216 | tf_op jit(solution)/shard_map/reshape | solution.py:33
  259.9 0.0 reduce-scatter.2.cloned.1.call-update
  260.0 79.8 %reduce-scatter.2.cloned.1.call-done = f32[256,2048]{1,0:T(8,128)} async-done(((f32[256,8192]{1,0:T(8,128)}), f32[256,2048]{1,0:T(8,128)}) %reduce-scatter.2.cloned.1.call-update) | async-done | bytes 2097168 | tf_op jit(solution)/shard_map/reduce_scatter | solution.py:34
  339.8 3.2 and_select_fusion.1
  (1 shorter events, 0.0 us)
Async XLA Ops:
  12.8 13.5 %copy-start.6 = (s32[64]{0:T(128)S(1)}, s32[64]{0:T(128)}, u32[]{:S(2)}) copy-start(s32[64]{0:T(128)} %param.8) | copy-start | bytes 772
  12.8 14.8 %copy-start.3 = (s32[64]{0:T(128)S(1)}, s32[64]{0:T(128)}, u32[]{:S(2)}) copy-start(s32[64]{0:T(128)} %param.9) | copy-start | bytes 772
  12.8 14.9 %copy-start.5 = (bf16[4,1,256,256]{3,2,1,0:T(8,128)(2,1)S(1)}, bf16[4,1,256,256]{3,2,1,0:T(8,128)(2,1)}, u32[]{:S(2)}) copy-start(bf16[4,1,256,256]{3,2,1,0:T(8,128)(2,1)} %param.6) | copy-start | bytes 1572868
  12.8 199.0 %all-to-all-start = ((bf16[64,4,1,128,128]{4,3,2,1,0:T(8,128)(2,1)}), bf16[64,4,1,128,128]{4,3,2,1,0:T(8,128)(2,1)}, u32[]{:S(2)}, u32[]{:S(2)}) async-start(bf16[64,4,1,128,128]{4,3,2,1,0:T(8,128)(2,1)} %stack.2), calls=%async_computation | async-start | bytes 16777216 | tf_op jit(solution)/shard_map/all_to_all | solution.py:24
  26.1 313.7 %reduce-scatter.2.cloned.1.call-start = ((), (), s32[]{:S(2)}) async-start(), calls=%async_computation.2 | async-start | bytes 10485760 | tf_op jit(solution)/shard_map/reduce_scatter | solution.py:34
  27.7 6.2 %copy-start.4 = (bf16[256,8192]{1,0:T(8,128)(2,1)S(1)}, bf16[256,8192]{1,0:T(8,128)(2,1)}, u32[]{:S(2)}) copy-start(bf16[256,8192]{1,0:T(8,128)(2,1)} %param.5) | copy-start | bytes 12582916
  222.2 5.2 %copy-start = (bf16[64,4,1,128,128]{4,3,0,2,1:T(8,128)(2,1)S(1)}, bf16[64,4,1,128,128]{4,3,0,2,1:T(8,128)(2,1)}, u32[]{:S(2)}) copy-start(bf16[64,4,1,128,128]{4,3,0,2,1:T(8,128)(2,1)} %copy.22) | copy-start | bytes 25165828
  222.2 6.4 %copy-start.2 = (bf16[8192,256]{1,0:T(8,128)(2,1)S(1)}, bf16[8192,256]{1,0:T(8,128)(2,1)}, u32[]{:S(2)}) copy-start(bf16[8192,256]{1,0:T(8,128)(2,1)} %convolution_convert_fusion.3) | copy-start | bytes 12582916
  228.6 4.5 %copy-start.1 = (bf16[8192,256]{1,0:T(8,128)(2,1)S(1)}, bf16[8192,256]{1,0:T(8,128)(2,1)}, u32[]{:S(2)}) copy-start(bf16[8192,256]{1,0:T(8,128)(2,1)} %convolution_convert_fusion.1) | copy-start | bytes 12582916
Sparse Core Ops, SparseCore 0:
  260.1 79.6 reduce-scatter.1
